TPU v7x, 32 devices: a whole 2x2x4 slice. The times are simulated.
32 devices in a mesh: groups: 2 (over y), roll: 4 (over z), tp: 2 (over x), seq: 2 (over core).
Axes of the slice: x: 2, y: 2, z: 4, core: 2. Of those that a mesh axis runs over, the one named last changes fastest.
Arguments:
- hidden: bfloat16 [128, 8192], P('groups', ('roll', 'seq')), parts along dimension 0, may hold values from -6 to 6
- w_query: bfloat16 [8192, 8192], P(('roll', 'seq'), 'tp'), may hold values from -0.0625 to 0.0625
- w_key: bfloat16 [8192, 1024], P(('roll', 'seq'), 'tp'), may hold values from -0.0625 to 0.0625
- w_value: bfloat16 [8192, 1024], P(('roll', 'seq'), 'tp'), may hold values from -0.0625 to 0.0625
- b_query: bfloat16 [8192], P('tp'), may hold values from -12 to 12
- b_key: bfloat16 [1024], P('tp'), may hold values from -12 to 12
- b_value: bfloat16 [1024], P('tp'), may hold values from -6 to 6
- w_out: bfloat16 [8192, 8192], P('tp', ('roll', 'seq')), may hold values from -0.0625 to 0.0625
- prefix_keys: bfloat16 [4, 4096, 1024], P('groups', ('roll', 'seq'), 'tp'), parts along dimension 0, may hold values from -256 to 256
- prefix_values: bfloat16 [4, 4096, 1024], P('groups', ('roll', 'seq'), 'tp'), parts along dimension 0, may hold values from -6 to 6
- suffix_keys: bfloat16 [16, 2048, 1024], P(('groups', 'roll'), 'seq', 'tp'), parts along dimension 0, may hold values from -6 to 6
- suffix_values: bfloat16 [16, 2048, 1024], P(('groups', 'roll'), 'seq', 'tp'), parts along dimension 0, may hold values from -6 to 6
- suffix_lengths: int32 [16], P('groups'), parts along dimension 0, may hold values from 1 to 2048, 8192 in all
- prompt_of: int32 [16], P('groups'), parts along dimension 0, may hold values from 0 to 1, as said below
Outputs:
- attended: bfloat16 [128, 8192], P(('groups', 'tp'), ('roll', 'seq')), parts along dimension 0
There are 2 independent parts, one for each index of `groups`. A program takes and returns all parts, laid end to end along the dimension named above; an argument that names none is the same for every part. Nothing has to cross between parts.
Inputs may be any that keep to these rules, and one draw needn't show every extreme that they name: Only the first suffix_lengths[r] rows of a rollout's suffix cache are live; the lengths of a group add up to 8192 and the largest is exactly 2048. `prompt_of`: every prompt is extended by exactly 4 rollouts.
All inputs are finite; a program needn't handle non-finite values.
Results may differ from a plain program's by a relative error of at most 0.009.
The roundings to bfloat16 on the way count: a program that leaves them out, or rounds other values in their place, can miss the bound.
Values may be sent and summed in bfloat16 or wider, within the bound.
No kernel may reach another device: no remote copies, remote signals or barrier semaphores. Data moves between devices by JAX's collectives and lax.ppermute only.
A program may use at most 128 MiB of HBM per device.

v0:
```python
import math
import jax
import jax.numpy as jnp
from jax import lax
from jax.sharding import PartitionSpec as P

HD = 128
GUESS = 8
ROPE_BASE = 1000000.0
NEG_FILL = -1e30


def rotate(values, positions):
    half = values.shape[-1] // 2
    steps = jnp.arange(half).astype(jnp.float32) * (2.0 / values.shape[-1])
    freqs = jnp.exp(-math.log(ROPE_BASE) * steps)
    angles = positions[:, None] * freqs[None, :]
    cosine = jnp.cos(angles)[:, None, :]
    sine = jnp.sin(angles)[:, None, :]
    first = values[..., :half]
    second = values[..., half:]
    return jnp.concatenate(
        [first * cosine - second * sine, second * cosine + first * sine], axis=-1
    )


def lookup(table, indices):
    hits = indices[:, None] == jnp.arange(table.shape[0], dtype=jnp.int32)[None, :]
    return jnp.sum(jnp.where(hits, table[None, :], 0), axis=1)


def combine(first, second):
    peak_a, total_a, numer_a = first
    peak_b, total_b, numer_b = second
    peak = jnp.maximum(peak_a, peak_b)
    factor_a = jnp.exp(peak_a - peak)
    factor_b = jnp.exp(peak_b - peak)
    return (
        peak,
        total_a * factor_a + total_b * factor_b,
        numer_a * factor_a[..., None] + numer_b * factor_b[..., None],
    )


def masked_stats(scores, visible, values):
    peak = jnp.max(jnp.where(visible, scores, NEG_FILL), axis=-1)
    weights = jnp.exp(jnp.where(visible, scores - peak[..., None], NEG_FILL))
    total = jnp.sum(weights, axis=-1)
    numer = jnp.einsum(
        "rtkgs,rskd->rtkgd",
        weights.astype(jnp.bfloat16),
        values,
        preferred_element_type=jnp.float32,
    )
    return (peak, total, numer)


def body(
    hidden,
    w_query,
    w_key,
    w_value,
    b_query,
    b_key,
    b_value,
    w_out,
    prefix_keys,
    prefix_values,
    suffix_keys,
    suffix_values,
    suffix_lengths,
    prompt_of,
):
    row_count = hidden.shape[0]
    q_heads = w_query.shape[1] // HD
    kv_heads = w_key.shape[1] // HD
    group = q_heads // kv_heads
    prompts = prefix_keys.shape[0]
    pre_dev = prefix_keys.shape[1]
    prefix_total = pre_dev * lax.axis_size(("roll", "seq"))
    per_device = suffix_keys.shape[0]
    suf_dev = suffix_keys.shape[1]
    scale = 1.0 / math.sqrt(HD)
    q_part = jnp.dot(hidden, w_query, preferred_element_type=jnp.float32)
    k_part = jnp.dot(hidden, w_key, preferred_element_type=jnp.float32)
    v_part = jnp.dot(hidden, w_value, preferred_element_type=jnp.float32)
    q_sum, k_sum, v_sum = lax.psum((q_part, k_part, v_part), ("roll", "seq"))
    count = q_sum.shape[0]
    row_ids = jnp.arange(count, dtype=jnp.int32)
    owner_ids = row_ids // GUESS
    positions = (prefix_total + lookup(suffix_lengths, owner_ids) + row_ids % GUESS).astype(
        jnp.float32
    )
    q_rot = rotate((q_sum + b_query.astype(jnp.float32)).reshape(count, q_heads, HD), positions)
    k_rot = rotate((k_sum + b_key.astype(jnp.float32)).reshape(count, kv_heads, HD), positions)
    v_fin = (v_sum + b_value.astype(jnp.float32)).reshape(count, kv_heads, HD)
    query = q_rot.astype(jnp.bfloat16)
    key_new = k_rot.astype(jnp.bfloat16)
    value_new = v_fin.astype(jnp.bfloat16)
    query_grid = query.reshape(row_count, kv_heads, group, HD)
    owners_all = jnp.arange(row_count, dtype=jnp.int32) // GUESS
    row_prompt = lookup(prompt_of, owners_all)
    pre_keys = prefix_keys.reshape(prompts, pre_dev, kv_heads, HD)
    pre_values = prefix_values.reshape(prompts, pre_dev, kv_heads, HD)
    peak_all = jnp.full((row_count, kv_heads, group), NEG_FILL, jnp.float32)
    total_all = jnp.zeros((row_count, kv_heads, group), jnp.float32)
    numer_all = jnp.zeros((row_count, kv_heads, group, HD), jnp.float32)
    for prompt in range(prompts):
        scores = (
            jnp.einsum(
                "tkgd,skd->tkgs", query_grid, pre_keys[prompt], preferred_element_type=jnp.float32
            )
            * scale
        )
        block_peak = jnp.max(scores, axis=-1)
        weights = jnp.exp(scores - block_peak[..., None])
        block_numer = jnp.einsum(
            "tkgs,skd->tkgd",
            weights.astype(jnp.bfloat16),
            pre_values[prompt],
            preferred_element_type=jnp.float32,
        )
        picked = (row_prompt == prompt)[:, None, None]
        peak_all = jnp.where(picked, block_peak, peak_all)
        total_all = jnp.where(picked, jnp.sum(weights, axis=-1), total_all)
        numer_all = jnp.where(picked[..., None], block_numer, numer_all)
    first_rollout = lax.axis_index("roll") * per_device
    seq_index = lax.axis_index("seq")
    local_len = lax.dynamic_slice_in_dim(suffix_lengths, first_rollout, per_device, 0)
    live = jnp.clip(local_len - seq_index * suf_dev, 0, suf_dev)
    row_start = first_rollout * GUESS
    local_rows = per_device * GUESS
    query_local = lax.dynamic_slice_in_dim(query_grid, row_start, local_rows, 0).reshape(
        per_device, GUESS, kv_heads, group, HD
    )
    suf_keys = suffix_keys.reshape(per_device, suf_dev, kv_heads, HD)
    suf_values = suffix_values.reshape(per_device, suf_dev, kv_heads, HD)
    scores = (
        jnp.einsum("rtkgd,rskd->rtkgs", query_local, suf_keys, preferred_element_type=jnp.float32)
        * scale
    )
    visible = (jnp.arange(suf_dev, dtype=jnp.int32)[None, :] < live[:, None])[
        :, None, None, None, :
    ]
    suffix_part = masked_stats(scores, visible, suf_values)
    key_local = lax.dynamic_slice_in_dim(key_new, row_start, local_rows, 0).reshape(
        per_device, GUESS, kv_heads, HD
    )
    value_local = lax.dynamic_slice_in_dim(value_new, row_start, local_rows, 0).reshape(
        per_device, GUESS, kv_heads, HD
    )
    new_scores = (
        jnp.einsum("rtkgd,rskd->rtkgs", query_local, key_local, preferred_element_type=jnp.float32)
        * scale
    )
    guess_ids = jnp.arange(GUESS, dtype=jnp.int32)
    causal = (guess_ids[None, :] <= guess_ids[:, None]) & (seq_index == 0)
    guess_part = masked_stats(new_scores, causal[None, :, None, None, :], value_local)
    prefix_local = (
        lax.dynamic_slice_in_dim(peak_all, row_start, local_rows, 0).reshape(
            per_device, GUESS, kv_heads, group
        ),
        lax.dynamic_slice_in_dim(total_all, row_start, local_rows, 0).reshape(
            per_device, GUESS, kv_heads, group
        ),
        lax.dynamic_slice_in_dim(numer_all, row_start, local_rows, 0).reshape(
            per_device, GUESS, kv_heads, group, HD
        ),
    )
    peak_loc, total_loc, numer_loc = combine(combine(prefix_local, suffix_part), guess_part)
    peak_all = lax.dynamic_update_slice_in_dim(
        peak_all, peak_loc.reshape(local_rows, kv_heads, group), row_start, 0
    )
    total_all = lax.dynamic_update_slice_in_dim(
        total_all, total_loc.reshape(local_rows, kv_heads, group), row_start, 0
    )
    numer_all = lax.dynamic_update_slice_in_dim(
        numer_all, numer_loc.reshape(local_rows, kv_heads, group, HD), row_start, 0
    )
    peaks, totals, numers = (
        lax.all_to_all(peak_all[None], ("roll", "seq"), split_axis=1, concat_axis=0, tiled=True),
        lax.all_to_all(total_all[None], ("roll", "seq"), split_axis=1, concat_axis=0, tiled=True),
        lax.all_to_all(numer_all[None], ("roll", "seq"), split_axis=1, concat_axis=0, tiled=True),
    )
    peak_top = jnp.max(peaks, axis=0)
    factors = jnp.exp(peaks - peak_top[None])
    share = (
        jnp.sum(numers * factors[..., None], axis=0) / jnp.sum(totals * factors, axis=0)[..., None]
    )
    share = share.astype(jnp.bfloat16).reshape(share.shape[0], q_heads * HD)
    attention = lax.all_gather(share, ("roll", "seq"), axis=0, tiled=True)
    summed = lax.psum_scatter(
        jnp.dot(attention, w_out, preferred_element_type=jnp.float32),
        "tp",
        scatter_dimension=0,
        tiled=True,
    )
    return summed.astype(jnp.bfloat16)


def solution(mesh):
    return jax.shard_map(
        body,
        mesh=mesh,
        in_specs=(
            P("groups", ("roll", "seq")),
            P(("roll", "seq"), "tp"),
            P(("roll", "seq"), "tp"),
            P(("roll", "seq"), "tp"),
            P("tp"),
            P("tp"),
            P("tp"),
            P("tp", ("roll", "seq")),
            P("groups", ("roll", "seq"), "tp"),
            P("groups", ("roll", "seq"), "tp"),
            P(("groups", "roll"), "seq", "tp"),
            P(("groups", "roll"), "seq", "tp"),
            P("groups"),
            P("groups"),
        ),
        out_specs=P(("groups", "tp"), ("roll", "seq")),
        check_vma=False,
    )
```

profile of v0, /device:TPU:0, one launch (start us, length us, event | category | flops | bytes accessed | tf_op | source)
XLA Modules:
  0.0 188.1 jit_solution(5365839674309538938)
XLA Ops:
  6.6 6.2 %fusion.91 = f32[64,4096]{1,0:T(8,128)} fusion(bf16[64,1024]{1,0:T(8,128)(2,1)} %param.14, bf16[1024,4096]{1,0:T(8,128)(2,1)} %param.15), kind=kOutput, calls=%fused_computation.143 | convolution fusion | flops 536870912 | bytes 9568256 | tf_op jit(solution)/shard_map/dot_general | solution.py:84
  12.8 1.0 fusion.92
  13.8 0.9 fusion.93
  15.0 0.2 copy.242
  15.2 0.2 copy.244
  15.5 4.0 %reshape.290 = bf16[2,1024,4,128]{3,2,1,0:T(4,128)(2,1)} reshape(bf16[2,1024,512]{2,1,0:T(8,128)(2,1)} %param.24) | data formatting | bytes 4194304 | tf_op jit(solution)/shard_map/reshape | solution.py:136
  19.5 0.6 dynamic-slice.4
  20.2 0.6 dynamic-slice.5
  20.8 1.3 fusion.89
  22.0 1.0 copy.245
  23.1 1.0 copy.243
  24.1 4.0 %reshape.291 = bf16[2,1024,4,128]{3,2,1,0:T(4,128)(2,1)} reshape(bf16[2,1024,512]{2,1,0:T(8,128)(2,1)} %param.25) | data formatting | bytes 4194304 | tf_op jit(solution)/shard_map/reshape | solution.py:137
  28.3 0.2 multiply_cosine_fusion
  28.5 49.9 %all-reduce.3.cloned.1.call-done = (f32[64,4096]{1,0:T(8,128)}, f32[64,512]{1,0:T(8,128)}, f32[64,512]{1,0:T(8,128)}) async-done(((f32[64,4096]{1,0:T(8,128)}, f32[64,512]{1,0:T(8,128)}, f32[64,512]{1,0:T(8,128)}), (f32[64,4096]{1,0:T(8,128)}, f32[64,512]{1,0:T(8,128)}, f32[64,512]{1,0:T(8,128)})) %all-reduce.3.cloned.1.call-update) | async-done | bytes 1310736 | tf_op jit(solution)/shard_map/psum | solution.py:87
  78.4 1.3 add_bitcast_fusion
  79.7 0.2 copy.249
  80.0 0.1 fusion.90
  80.2 0.5 fusion.50
  80.7 0.1 constant_dynamic-slice_fusion.1
  80.8 0.9 bitcast_reduce_fusion.1
  81.6 0.9 bitcast_reduce_fusion
  82.6 0.7 select_reduce_fusion
  83.3 0.2 fusion.52
  83.5 1.1 copy-done.6
  84.6 2.3 %fusion.2 = (f32[64,4,8]{2,0,1:T(8,128)S(1)}, f32[64,4,8]{2,0,1:T(8,128)S(1)}) fusion(f32[4,64,8,512]{3,2,1,0:T(8,128)S(1)} %get-tuple-element.37, f32[64,4,8]{2,0,1:T(8,128)S(1)} %get-tuple-element.36, f32[64,4,8]{2,0,1:T(8,128)S(1)} %get-tuple-element.34, f32[4,64,8,512]{3,2,1,0:T(8,128)S(1)} %get-tuple-element.35), kind=kLoop, calls=%fused_computation.6 | loop fusion | flops 6287360 | bytes 8421376 | tf_op jit(solution)/shard_map/reduce_sum | solution.py:125
  87.0 0.1 fusion.56
  87.1 0.9 fusion.12
  88.0 0.6 fusion.21
  88.6 0.1 fusion.69
  88.8 0.7 fusion.63
  89.5 0.7 copy.324
  90.2 1.7 reshape.303
  91.9 3.5 %all-to-all-start.1 = ((f32[8,1,256]{2,1,0:T(1,128)}), f32[8,1,256]{2,1,0:T(1,128)S(1)}, u32[]{:S(2)}, u32[]{:S(2)}) async-start(f32[8,1,256]{2,1,0:T(1,128)} %reshape.303), calls=%async_computation.1 | async-start | bytes 16384 | tf_op jit(solution)/shard_map/all_to_all | solution.py:181
  95.3 3.2 %fusion.26 = f32[4,64,8,128]{3,2,1,0:T(8,128)S(1)} fusion(bf16[512,4,128,1]{0,2,3,1:T(8,128)(2,1)} %bitcast.189, f32[4,64,8,512]{3,2,1,0:T(8,128)} %copy-done.3, f32[64,4,8]{2,0,1:T(8,128)S(1)} %get-tuple-element.34, pred[64]{0:T(512)(128)(4,1)} %copy-done.20), kind=kOutput, calls=%fused_computation.28 | convolution fusion | flops 271843328 | bytes 5775424 | tf_op jit(solution)/shard_map/tkgs,skd->tkgd/dot_general | solution.py:117
  98.5 0.4 copy-done.2
  98.9 0.1 copy-done.8
  99.1 1.6 fusion.23
  100.6 1.0 copy-done.5
  101.6 0.7 constant_dynamic-slice_fusion.2
  102.3 0.6 convert_element_type.64
  103.0 0.8 constant_dynamic-slice_fusion
  103.7 2.6 %fusion.41 = f32[2,8,4,8,128]{4,3,1,2,0:T(8,128)S(1)} fusion(bf16[2,1024,4,128,1]{3,2,1,0,4:T(4,128)(2,1)} %bitcast.192, f32[2,4,8,8,1024]{4,3,2,1,0:T(8,128)S(1)} %get-tuple-element.39, f32[2,8,4,8]{3,1,2,0:T(8,128)S(1)} %get-tuple-element.38, pred[2,1024]{1,0:T(4,128)(4,1)S(1)} %iota_compare_fusion, f32[2,8,4,8,128]{4,3,1,0,2:T(8,128)} %bitcast.202, ...), kind=kOutput, calls=%fused_computation.37 | convolution fusion | flops 136577024 | bytes 4728832 | tf_op jit(solution)/shard_map/rtkgs,rskd->rtkgd/dot_general | solution.py:49
  106.3 0.3 fusion.34
  106.8 0.8 reshape.305
  107.6 4.9 %all-to-all-start.2 = ((f32[8,1,256]{2,1,0:T(1,128)}), f32[8,1,256]{2,1,0:T(1,128)S(1)}, u32[]{:S(2)}, u32[]{:S(2)}) async-start(f32[8,1,256]{2,1,0:T(1,128)} %reshape.305), calls=%async_computation.2 | async-start | bytes 16384 | tf_op jit(solution)/shard_map/all_to_all | solution.py:182
  112.4 0.7 constant_dynamic-update-slice_fusion
  113.1 2.4 %copy.197 = f32[1,64,4,8,128]{4,3,2,0,1:T(8,128)} copy(f32[1,64,4,8,128]{4,3,1,2,0:T(8,128)} %constant_dynamic-update-slice_fusion) | data formatting | bytes 2097152 | tf_op jit(solution)/shard_map/dynamic_update_slice | solution.py:177
  115.5 2.5 %all-to-all-done.2 = f32[8,1,256]{2,1,0:T(1,128)S(1)} async-done(((f32[8,1,256]{2,1,0:T(1,128)}), f32[8,1,256]{2,1,0:T(1,128)S(1)}, u32[]{:S(2)}, u32[]{:S(2)}) %all-to-all-start.2) | async-done | bytes 8224 | tf_op jit(solution)/shard_map/all_to_all | solution.py:182
  118.0 3.6 %all-to-all-start = ((f32[1,64,4,8,128]{4,3,2,0,1:T(8,128)}), f32[1,64,4,8,128]{4,3,2,0,1:T(8,128)S(1)}, u32[]{:S(2)}, u32[]{:S(2)}) async-start(f32[1,64,4,8,128]{4,3,2,0,1:T(8,128)} %copy.197), calls=%async_computation | async-start | bytes 2097152 | tf_op jit(solution)/shard_map/all_to_all | solution.py:183
  121.7 0.5 broadcast.227
  122.2 0.7 reduce.1
  122.8 0.2 reshape.304
  123.0 0.1 copy.202
  123.3 0.7 reduce
  124.0 0.2 reshape.306
  124.2 0.1 copy.208
  124.4 0.1 copy.203
  124.5 23.6 %all-to-all-done = f32[1,64,4,8,128]{4,3,2,0,1:T(8,128)S(1)} async-done(((f32[1,64,4,8,128]{4,3,2,0,1:T(8,128)}), f32[1,64,4,8,128]{4,3,2,0,1:T(8,128)S(1)}, u32[]{:S(2)}, u32[]{:S(2)}) %all-to-all-start) | async-done | bytes 1048608 | tf_op jit(solution)/shard_map/all_to_all | solution.py:183
  148.1 0.3 fusion.45
  148.4 0.1 copy_bitcast_fusion.1
  148.6 14.9 %all_gather.3 = bf16[64,4096]{1,0:T(8,128)(2,1)S(1)} all-gather(bf16[8,4096]{1,0:T(8,128)(2,1)S(1)} %bitcast.203), channel_id=1, replica_groups=mesh['groups'=2,'roll'=4,'tp'=2,'seq'=2] {'roll','seq'}, dimensions={0}, use_global_device_ids=true | all-gather | bytes 589824 | tf_op jit(solution)/shard_map/all_gather | solution.py:191
  163.5 5.7 %fusion.94 = f32[64,1024]{1,0:T(8,128)} fusion(bf16[64,4096]{1,0:T(8,128)(2,1)S(1)} %all_gather.3, bf16[4096,1024]{1,0:T(8,128)(2,1)} %param.21), kind=kOutput, calls=%fused_computation.146 | convolution fusion | flops 536870912 | bytes 9175040 | tf_op jit(solution)/shard_map/dot_general | solution.py:193
  169.2 10.6 %reduce-scatter.2.cloned.1.call-done = f32[32,1024]{1,0:T(8,128)} async-done(((f32[64,1024]{1,0:T(8,128)}), f32[32,1024]{1,0:T(8,128)}) %reduce-scatter.2.cloned.1.call-update) | async-done | bytes 131088 | tf_op jit(solution)/shard_map/reduce_scatter | solution.py:192
  179.7 1.5 convert_element_type.68
  (80 shorter events, 1.1 us)
Async XLA Ops:
  6.5 6.3 %copy-start = (bf16[1024,512]{1,0:T(8,128)(2,1)S(1)}, bf16[1024,512]{1,0:T(8,128)(2,1)}, u32[]{:S(2)}) copy-start(bf16[1024,512]{1,0:T(8,128)(2,1)} %param.16) | copy-start | bytes 3145732
  6.5 6.3 %copy-start.9 = (bf16[64,1024]{1,0:T(8,128)(2,1)S(1)}, bf16[64,1024]{1,0:T(8,128)(2,1)}, u32[]{:S(2)}) copy-start(bf16[64,1024]{1,0:T(8,128)(2,1)} %param.14) | copy-start | bytes 393220
  6.5 7.2 %copy-start.10 = (bf16[1024,512]{1,0:T(8,128)(2,1)S(1)}, bf16[1024,512]{1,0:T(8,128)(2,1)}, u32[]{:S(2)}) copy-start(bf16[1024,512]{1,0:T(8,128)(2,1)} %param.17) | copy-start | bytes 3145732
  6.5 8.2 %copy-start.17 = (bf16[4096]{0:T(1024)(128)(2,1)S(1)}, bf16[4096]{0:T(1024)(128)(2,1)}, u32[]{:S(2)}) copy-start(bf16[4096]{0:T(1024)(128)(2,1)} %param.18) | copy-start | bytes 24580
  6.5 8.3 %copy-start.23 = (bf16[512]{0:T(512)(128)(2,1)S(1)}, bf16[512]{0:T(512)(128)(2,1)}, u32[]{:S(2)}) copy-start(bf16[512]{0:T(512)(128)(2,1)} %param.19) | copy-start | bytes 3076
  6.5 8.3 %copy-start.24 = (bf16[512]{0:T(512)(128)(2,1)S(1)}, bf16[512]{0:T(512)(128)(2,1)}, u32[]{:S(2)}) copy-start(bf16[512]{0:T(512)(128)(2,1)} %param.20) | copy-start | bytes 3076
  6.6 71.8 %all-reduce.3.cloned.1.call-start = ((), (), s32[]{:S(2)}) async-start(), calls=%async_computation.5 | async-start | bytes 2621440 | tf_op jit(solution)/shard_map/psum | solution.py:87
  12.8 2.1 %copy-start.11 = (bf16[2,512,512]{2,1,0:T(8,128)(2,1)S(1)}, bf16[2,512,512]{2,1,0:T(8,128)(2,1)}, u32[]{:S(2)}) copy-start(bf16[2,512,512]{2,1,0:T(8,128)(2,1)} %param.22) | copy-start | bytes 3145732
  12.8 2.6 %copy-start.22 = (s32[8]{0:T(128)S(1)}, s32[8]{0:T(128)}, u32[]{:S(2)}) copy-start(s32[8]{0:T(128)} %param.26) | copy-start | bytes 100
  12.8 2.6 %copy-start.27 = (s32[8]{0:T(128)S(1)}, s32[8]{0:T(128)}, u32[]{:S(2)}) copy-start(s32[8]{0:T(128)} %param.27) | copy-start | bytes 100
  15.5 8.6 %copy-start.18 = (pred[64]{0:T(512)(128)(4,1)}, pred[64]{0:T(512)(128)(4,1)S(1)}, u32[]{:S(2)}) copy-start(pred[64]{0:T(512)(128)(4,1)S(1)} %get-tuple-element.32) | copy-start | bytes 196
  15.5 8.6 %copy-start.20 = (pred[64]{0:T(512)(128)(4,1)}, pred[64]{0:T(512)(128)(4,1)S(1)}, u32[]{:S(2)}) copy-start(pred[64]{0:T(512)(128)(4,1)S(1)} %get-tuple-element.33) | copy-start | bytes 196
  78.4 1.5 copy-start.14
  78.4 1.6 copy-start.15
  81.6 5.3 %copy-start.1 = (f32[4,64,8,512]{3,2,1,0:T(8,128)}, f32[4,64,8,512]{3,2,1,0:T(8,128)S(1)}, u32[]{:S(2)}) copy-start(f32[4,64,8,512]{3,2,1,0:T(8,128)S(1)} %get-tuple-element.37) | copy-start | bytes 12582916
  82.5 4.4 %copy-start.3 = (f32[4,64,8,512]{3,2,1,0:T(8,128)}, f32[4,64,8,512]{3,2,1,0:T(8,128)S(1)}, u32[]{:S(2)}) copy-start(f32[4,64,8,512]{3,2,1,0:T(8,128)S(1)} %get-tuple-element.35) | copy-start | bytes 12582916
  83.3 1.3 copy-start.6
  84.6 2.3 %copy-start.19 = (pred[64]{0:T(512)(128)(4,1)S(1)}, pred[64]{0:T(512)(128)(4,1)}, u32[]{:S(2)}) copy-start(pred[64]{0:T(512)(128)(4,1)} %copy-done.18) | copy-start | bytes 196
  84.6 2.4 %copy-start.21 = (pred[64]{0:T(512)(128)(4,1)S(1)}, pred[64]{0:T(512)(128)(4,1)}, u32[]{:S(2)}) copy-start(pred[64]{0:T(512)(128)(4,1)} %copy-done.20) | copy-start | bytes 196
  84.6 2.5 %copy-start.4 = (bf16[2,1024,4,128]{3,2,1,0:T(4,128)(2,1)S(1)}, bf16[2,1024,4,128]{3,2,1,0:T(4,128)(2,1)}, u32[]{:S(2)}) copy-start(bf16[2,1024,4,128]{3,2,1,0:T(4,128)(2,1)} %reshape.290) | copy-start | bytes 6291460
  86.9 1.7 copy-start.25
  86.9 1.7 copy-start.26
  88.7 1.5 copy-start.12
  91.9 15.7 %all-to-all-start.1 = ((f32[8,1,256]{2,1,0:T(1,128)}), f32[8,1,256]{2,1,0:T(1,128)S(1)}, u32[]{:S(2)}, u32[]{:S(2)}) async-start(f32[8,1,256]{2,1,0:T(1,128)} %reshape.303), calls=%async_computation.1 | async-start | bytes 16384 | tf_op jit(solution)/shard_map/all_to_all | solution.py:181
  95.3 3.6 %copy-start.2 = (f32[4,64,8,512]{3,2,1,0:T(8,128)S(1)}, f32[4,64,8,512]{3,2,1,0:T(8,128)}, u32[]{:S(2)}) copy-start(f32[4,64,8,512]{3,2,1,0:T(8,128)} %copy-done.1) | copy-start | bytes 12582916
  95.3 3.7 %copy-start.8 = (bf16[1,512,512]{1,2,0:T(8,128)(2,1)S(1)}, bf16[1,512,512]{1,2,0:T(8,128)(2,1)}, u32[]{:S(2)}) copy-start(bf16[1,512,512]{1,2,0:T(8,128)(2,1)} %copy.243) | copy-start | bytes 1572868
  100.6 1.0 copy-start.5
  101.6 4.7 %copy-start.7 = (f32[2,8,4,8,8]{3,4,1,2,0:T(8,128)S(1)}, f32[2,8,4,8,8]{3,4,1,2,0:T(8,128)}, u32[]{:S(2)}) copy-start(f32[2,8,4,8,8]{3,4,1,2,0:T(8,128)} %copy-done.6) | copy-start | bytes 49156
  103.0 3.4 %copy-start.16 = (f32[2,8,4,8]{3,1,2,0:T(8,128)S(1)}, f32[2,8,4,8]{3,1,2,0:T(8,128)}, u32[]{:S(2)}) copy-start(f32[2,8,4,8]{3,1,2,0:T(8,128)} %get-tuple-element.24) | copy-start | bytes 6148
  103.0 3.7 %copy-start.13 = (f32[1,64,4,8]{3,1,2,0:T(8,128)S(1)}, f32[1,64,4,8]{3,1,2,0:T(8,128)}, u32[]{:S(2)}) copy-start(f32[1,64,4,8]{3,1,2,0:T(8,128)} %copy-done.12) | copy-start | bytes 24580
  107.6 10.5 %all-to-all-start.2 = ((f32[8,1,256]{2,1,0:T(1,128)}), f32[8,1,256]{2,1,0:T(1,128)S(1)}, u32[]{:S(2)}, u32[]{:S(2)}) async-start(f32[8,1,256]{2,1,0:T(1,128)} %reshape.305), calls=%async_computation.2 | async-start | bytes 16384 | tf_op jit(solution)/shard_map/all_to_all | solution.py:182
  118.0 30.1 %all-to-all-start = ((f32[1,64,4,8,128]{4,3,2,0,1:T(8,128)}), f32[1,64,4,8,128]{4,3,2,0,1:T(8,128)S(1)}, u32[]{:S(2)}, u32[]{:S(2)}) async-start(f32[1,64,4,8,128]{4,3,2,0,1:T(8,128)} %copy.197), calls=%async_computation | async-start | bytes 2097152 | tf_op jit(solution)/shard_map/all_to_all | solution.py:183
  121.6 58.1 %reduce-scatter.2.cloned.1.call-start = ((), (), s32[]{:S(2)}) async-start(), calls=%async_computation.4 | async-start | bytes 393216 | tf_op jit(solution)/shard_map/reduce_scatter | solution.py:192
Sparse Core Ops, SparseCore 0:
  14.9 63.4 all-reduce.2
  169.3 10.3 reduce-scatter.1
where the time goes:
time: 189 us; the launch traced here: 188 us
  waiting for transfers between devices  86.6 us (46%)
  local copies, waits for them, and re-layouts  26 us (14%)
  matrix products  24.8 us (13%)
  blocking collectives  14.9 us (8%)
  between operations  14 us (7%)
  starting transfers between devices  11.9 us (6%)
  other arithmetic  9.87 us (5%)
    psum x1, waiting for transfers between devices, body(): q_sum, k_sum, v_sum = lax.psum((q_part, k_part, v_part), ('roll', 'seq'))  49.9 us
    all_to_all x1, waiting for transfers between devices, body(): lax.all_to_all(numer_all[None], ('roll', 'seq'), split_axis=1, concat_axi...  23.6 us
    all_gather x1, blocking collectives, body(): attention = lax.all_gather(share, ('roll', 'seq'), axis=0, tiled=True)  14.9 us
    reduce_scatter x1, waiting for transfers between devices, body(): lax.psum_scatter(jnp.dot(attention, w_out, preferred_element_type=jnp.flo...  10.6 us
    unnamed x66, local copies, waits for them, and re-layouts  8.2 us
    dot_general x1, matrix products, body(): q_part = jnp.dot(hidden, w_query, preferred_element_type=jnp.float32)  6.18 us
    dot_general x1, matrix products, body(): jnp.dot(attention, w_out, preferred_element_type=jnp.float32)  5.67 us
    all_to_all x1, starting transfers between devices, body(): lax.all_to_all(total_all[None], ('roll', 'seq'), split_axis=1, concat_axi...  4.86 us
  transfers between devices with their start and end apart: 5, of which 4 were waited for; matrix products, arithmetic and copies ran while one was open for 16% of the time, Pallas kernels for 0%

commit v1 on v0

--- a/solution.py
+++ b/solution.py
@@ -8,6 +8,18 @@
 GUESS = 8
 ROPE_BASE = 1000000.0
 NEG_FILL = -1e30
+
+
+def doubled_up(x, axis, dim):
+    ways, here = (lax.axis_size(axis), lax.axis_index(axis))
+    grown, reach = (x, 1)
+    while reach < ways:
+        theirs = lax.ppermute(grown, axis, [(d, d ^ reach) for d in range(ways)])
+        mine_first = jnp.concatenate([grown, theirs], axis=dim)
+        theirs_first = jnp.concatenate([theirs, grown], axis=dim)
+        grown = jnp.where(here & reach == 0, mine_first, theirs_first)
+        reach = 2 * reach
+    return grown
 
 
 def rotate(values, positions):
@@ -188,7 +200,7 @@
         jnp.sum(numers * factors[..., None], axis=0) / jnp.sum(totals * factors, axis=0)[..., None]
     )
     share = share.astype(jnp.bfloat16).reshape(share.shape[0], q_heads * HD)
-    attention = lax.all_gather(share, ("roll", "seq"), axis=0, tiled=True)
+    attention = doubled_up(share, ("roll", "seq"), 0)
     summed = lax.psum_scatter(
         jnp.dot(attention, w_out, preferred_element_type=jnp.float32),
         "tp",

time: 189 us -> 195 us (1.032)
  waiting for transfers between devices: 86.6 us -> 108 us
  blocking collectives: 14.9 us -> 0 us
    ppermute x0 -> x3, waiting for transfers between devices: none -> 20.7 us  [doubled_up(): theirs = lax.ppermute(grown, axis, [(d, d ^ reach) for d in range(ways)])]
    all_gather x1 -> x0, blocking collectives: 14.9 us -> none  [body(): attention = lax.all_gather(share, ('roll', 'seq'), axis=0, tiled=True)]
  transfers between devices with their start and end apart: 5 -> 8, of which waited for: 4 -> 7; matrix products, arithmetic and copies ran while one was open for 16% -> 15% of each run, Pallas kernels for 0% -> 0%
where the time goes in v1:
time: 195 us; the launch traced here: 194 us
  waiting for transfers between devices  108 us (55%)
  local copies, waits for them, and re-layouts  25.6 us (13%)
  matrix products  24.8 us (13%)
  between operations  14 us (7%)
  starting transfers between devices  12.2 us (6%)
  other arithmetic  9.96 us (5%)
    psum x1, waiting for transfers between devices, body(): q_sum, k_sum, v_sum = lax.psum((q_part, k_part, v_part), ('roll', 'seq'))  50 us
    all_to_all x1, waiting for transfers between devices, body(): lax.all_to_all(numer_all[None], ('roll', 'seq'), split_axis=1, concat_axi...  24 us
    ppermute x3, waiting for transfers between devices, doubled_up(): theirs = lax.ppermute(grown, axis, [(d, d ^ reach) for d in range(ways)])  20.7 us
    reduce_scatter x1, waiting for transfers between devices, body(): lax.psum_scatter(jnp.dot(attention, w_out, preferred_element_type=jnp.flo...  10.7 us
    unnamed x66, local copies, waits for them, and re-layouts  8.24 us
    dot_general x1, matrix products, body(): q_part = jnp.dot(hidden, w_query, preferred_element_type=jnp.float32)  6.16 us
    dot_general x1, matrix products, body(): jnp.dot(attention, w_out, preferred_element_type=jnp.float32)  5.66 us
    all_to_all x1, starting transfers between devices, body(): lax.all_to_all(total_all[None], ('roll', 'seq'), split_axis=1, concat_axi...  4.86 us
  transfers between devices with their start and end apart: 8, of which 7 were waited for; matrix products, arithmetic and copies ran while one was open for 15% of the time, Pallas kernels for 0%

profile of v1, /device:TPU:0, one launch (start us, length us, event | category | flops | bytes accessed | tf_op | source)
XLA Modules:
  0.0 194.5 jit_solution(2753239720130941171)
XLA Ops:
  6.6 6.2 %fusion.99 = f32[64,4096]{1,0:T(8,128)} fusion(bf16[64,1024]{1,0:T(8,128)(2,1)} %param.14, bf16[1024,4096]{1,0:T(8,128)(2,1)} %param.15), kind=kOutput, calls=%fused_computation.154 | convolution fusion | flops 536870912 | bytes 9568256 | tf_op jit(solution)/shard_map/dot_general | solution.py:96
  12.8 0.9 fusion.100
  13.8 1.0 fusion.101
  14.9 0.2 copy.230
  15.2 0.2 copy.232
  15.5 4.0 %reshape.290 = bf16[2,1024,4,128]{3,2,1,0:T(4,128)(2,1)} reshape(bf16[2,1024,512]{2,1,0:T(8,128)(2,1)} %param.24) | data formatting | bytes 4194304 | tf_op jit(solution)/shard_map/reshape | solution.py:148
  19.5 0.6 dynamic-slice.4
  20.0 0.7 dynamic-slice.5
  20.7 1.3 fusion.97
  22.0 1.0 copy.233
  23.0 1.0 copy.231
  24.0 4.0 %reshape.291 = bf16[2,1024,4,128]{3,2,1,0:T(4,128)(2,1)} reshape(bf16[2,1024,512]{2,1,0:T(8,128)(2,1)} %param.25) | data formatting | bytes 4194304 | tf_op jit(solution)/shard_map/reshape | solution.py:149
  28.2 0.2 multiply_cosine_fusion
  28.4 50.0 %all-reduce.3.cloned.1.call-done = (f32[64,4096]{1,0:T(8,128)}, f32[64,512]{1,0:T(8,128)}, f32[64,512]{1,0:T(8,128)}) async-done(((f32[64,4096]{1,0:T(8,128)}, f32[64,512]{1,0:T(8,128)}, f32[64,512]{1,0:T(8,128)}), (f32[64,4096]{1,0:T(8,128)}, f32[64,512]{1,0:T(8,128)}, f32[64,512]{1,0:T(8,128)})) %all-reduce.3.cloned.1.call-update) | async-done | bytes 1310736 | tf_op jit(solution)/shard_map/psum | solution.py:99
  78.4 1.3 add_bitcast_fusion
  79.7 0.2 copy.237
  80.0 0.1 fusion.98
  80.1 0.5 fusion.50
  80.6 0.1 constant_dynamic-slice_fusion.1
  80.7 0.9 bitcast_reduce_fusion.1
  81.6 0.9 bitcast_reduce_fusion
  82.5 0.7 select_reduce_fusion
  83.3 0.2 fusion.59
  83.5 1.1 copy-done.6
  84.6 2.3 %fusion.2 = (f32[64,4,8]{2,0,1:T(8,128)S(1)}, f32[64,4,8]{2,0,1:T(8,128)S(1)}) fusion(f32[4,64,8,512]{3,2,1,0:T(8,128)S(1)} %get-tuple-element.37, f32[64,4,8]{2,0,1:T(8,128)S(1)} %get-tuple-element.36, f32[64,4,8]{2,0,1:T(8,128)S(1)} %get-tuple-element.34, f32[4,64,8,512]{3,2,1,0:T(8,128)S(1)} %get-tuple-element.35), kind=kLoop, calls=%fused_computation.6 | loop fusion | flops 6287360 | bytes 8421376 | tf_op jit(solution)/shard_map/reduce_sum | solution.py:137
  86.9 0.1 fusion.63
  87.1 0.9 fusion.12
  88.0 0.6 fusion.21
  88.6 0.1 fusion.76
  88.7 0.7 fusion.70
  89.4 0.7 copy.312
  90.2 1.7 reshape.303
  91.8 3.4 %all-to-all-start.1 = ((f32[8,1,256]{2,1,0:T(1,128)}), f32[8,1,256]{2,1,0:T(1,128)S(1)}, u32[]{:S(2)}, u32[]{:S(2)}) async-start(f32[8,1,256]{2,1,0:T(1,128)} %reshape.303), calls=%async_computation.1 | async-start | bytes 16384 | tf_op jit(solution)/shard_map/all_to_all | solution.py:193
  95.3 3.2 %fusion.26 = f32[4,64,8,128]{3,2,1,0:T(8,128)S(1)} fusion(bf16[512,4,128,1]{0,2,3,1:T(8,128)(2,1)} %bitcast.188, f32[4,64,8,512]{3,2,1,0:T(8,128)} %copy-done.3, f32[64,4,8]{2,0,1:T(8,128)S(1)} %get-tuple-element.34, pred[64]{0:T(512)(128)(4,1)} %copy-done.20), kind=kOutput, calls=%fused_computation.28 | convolution fusion | flops 271843328 | bytes 5775424 | tf_op jit(solution)/shard_map/tkgs,skd->tkgd/dot_general | solution.py:129
  98.5 0.4 copy-done.2
  98.9 0.1 copy-done.8
  99.0 1.6 fusion.23
  100.6 1.0 copy-done.5
  101.6 0.7 constant_dynamic-slice_fusion.2
  102.3 0.6 convert_element_type.64
  103.0 0.8 constant_dynamic-slice_fusion
  103.7 2.6 %fusion.41 = f32[2,8,4,8,128]{4,3,1,2,0:T(8,128)S(1)} fusion(bf16[2,1024,4,128,1]{3,2,1,0,4:T(4,128)(2,1)} %bitcast.191, f32[2,4,8,8,1024]{4,3,2,1,0:T(8,128)S(1)} %get-tuple-element.39, f32[2,8,4,8]{3,1,2,0:T(8,128)S(1)} %get-tuple-element.38, pred[2,1024]{1,0:T(4,128)(4,1)S(1)} %iota_compare_fusion, f32[2,8,4,8,128]{4,3,1,0,2:T(8,128)} %bitcast.201, ...), kind=kOutput, calls=%fused_computation.37 | convolution fusion | flops 136577024 | bytes 4728832 | tf_op jit(solution)/shard_map/rtkgs,rskd->rtkgd/dot_general | solution.py:61
  106.3 0.3 fusion.34
  106.8 0.8 reshape.305
  107.6 4.9 %all-to-all-start.2 = ((f32[8,1,256]{2,1,0:T(1,128)}), f32[8,1,256]{2,1,0:T(1,128)S(1)}, u32[]{:S(2)}, u32[]{:S(2)}) async-start(f32[8,1,256]{2,1,0:T(1,128)} %reshape.305), calls=%async_computation.2 | async-start | bytes 16384 | tf_op jit(solution)/shard_map/all_to_all | solution.py:194
  112.4 0.7 constant_dynamic-update-slice_fusion
  113.2 2.4 %copy.188 = f32[1,64,4,8,128]{4,3,2,0,1:T(8,128)} copy(f32[1,64,4,8,128]{4,3,1,2,0:T(8,128)} %constant_dynamic-update-slice_fusion) | data formatting | bytes 2097152 | tf_op jit(solution)/shard_map/dynamic_update_slice | solution.py:189
  115.5 2.5 %all-to-all-done.2 = f32[8,1,256]{2,1,0:T(1,128)S(1)} async-done(((f32[8,1,256]{2,1,0:T(1,128)}), f32[8,1,256]{2,1,0:T(1,128)S(1)}, u32[]{:S(2)}, u32[]{:S(2)}) %all-to-all-start.2) | async-done | bytes 8224 | tf_op jit(solution)/shard_map/all_to_all | solution.py:194
  118.0 3.6 %all-to-all-start = ((f32[1,64,4,8,128]{4,3,2,0,1:T(8,128)}), f32[1,64,4,8,128]{4,3,2,0,1:T(8,128)S(1)}, u32[]{:S(2)}, u32[]{:S(2)}) async-start(f32[1,64,4,8,128]{4,3,2,0,1:T(8,128)} %copy.188), calls=%async_computation | async-start | bytes 2097152 | tf_op jit(solution)/shard_map/all_to_all | solution.py:195
  121.7 0.5 broadcast.227
  122.2 0.7 reduce.1
  122.8 0.2 reshape.304
  123.0 0.7 reduce
  123.7 0.2 reshape.306
  124.1 24.0 %all-to-all-done = f32[1,64,4,8,128]{4,3,2,0,1:T(8,128)S(1)} async-done(((f32[1,64,4,8,128]{4,3,2,0,1:T(8,128)}), f32[1,64,4,8,128]{4,3,2,0,1:T(8,128)S(1)}, u32[]{:S(2)}, u32[]{:S(2)}) %all-to-all-start) | async-done | bytes 1048608 | tf_op jit(solution)/shard_map/all_to_all | solution.py:195
  148.1 0.3 fusion.45
  148.4 0.1 copy_bitcast_fusion.1
  148.7 1.2 collective-permute-done
  150.0 5.5 %collective-permute-done.1 = bf16[16,4096]{1,0:T(8,128)(2,1)S(1)} collective-permute-done((bf16[16,4096]{1,0:T(8,128)(2,1)S(1)}, bf16[16,4096]{1,0:T(8,128)(2,1)S(1)}, u32[]{:S(2)}, u32[]{:S(2)}) %collective-permute-start.1) | collective-permute-done | bytes 131104 | tf_op jit(solution)/shard_map/ppermute | solution.py:17
  155.6 0.2 collective-permute-start.2
  155.8 13.9 %collective-permute-done.2 = bf16[32,4096]{1,0:T(8,128)(2,1)S(1)} collective-permute-done((bf16[32,4096]{1,0:T(8,128)(2,1)S(1)}, bf16[32,4096]{1,0:T(8,128)(2,1)S(1)}, u32[]{:S(2)}, u32[]{:S(2)}) %collective-permute-start.2) | collective-permute-done | bytes 262176 | tf_op jit(solution)/shard_map/ppermute | solution.py:17
  169.7 5.7 %fusion.52 = f32[64,1024]{1,0:T(8,128)} fusion(bf16[4096,1024]{1,0:T(8,128)(2,1)} %param.21, bf16[32,4096]{1,0:T(8,128)(2,1)S(1)} %collective-permute-done.2, bf16[32,4096]{1,0:T(8,128)(2,1)S(1)} %maximum_select_fusion.2, pred[]{:T(512)S(6)} %eq.64), kind=kOutput, calls=%fused_computation.51 | convolution fusion | flops 539230208 | bytes 9175041 | tf_op jit(solution)/shard_map/dot_general | solution.py:205
  175.4 10.7 %reduce-scatter.2.cloned.1.call-done = f32[32,1024]{1,0:T(8,128)} async-done(((f32[64,1024]{1,0:T(8,128)}), f32[32,1024]{1,0:T(8,128)}) %reduce-scatter.2.cloned.1.call-update) | async-done | bytes 131088 | tf_op jit(solution)/shard_map/reduce_scatter | solution.py:204
  186.1 1.5 convert_element_type.68
  (84 shorter events, 1.2 us)
Async XLA Ops:
  6.5 6.2 %copy-start = (bf16[1024,512]{1,0:T(8,128)(2,1)S(1)}, bf16[1024,512]{1,0:T(8,128)(2,1)}, u32[]{:S(2)}) copy-start(bf16[1024,512]{1,0:T(8,128)(2,1)} %param.16) | copy-start | bytes 3145732
  6.5 6.2 %copy-start.9 = (bf16[64,1024]{1,0:T(8,128)(2,1)S(1)}, bf16[64,1024]{1,0:T(8,128)(2,1)}, u32[]{:S(2)}) copy-start(bf16[64,1024]{1,0:T(8,128)(2,1)} %param.14) | copy-start | bytes 393220
  6.5 7.2 %copy-start.10 = (bf16[1024,512]{1,0:T(8,128)(2,1)S(1)}, bf16[1024,512]{1,0:T(8,128)(2,1)}, u32[]{:S(2)}) copy-start(bf16[1024,512]{1,0:T(8,128)(2,1)} %param.17) | copy-start | bytes 3145732
  6.5 8.2 %copy-start.17 = (bf16[4096]{0:T(1024)(128)(2,1)S(1)}, bf16[4096]{0:T(1024)(128)(2,1)}, u32[]{:S(2)}) copy-start(bf16[4096]{0:T(1024)(128)(2,1)} %param.18) | copy-start | bytes 24580
  6.5 8.2 %copy-start.23 = (bf16[512]{0:T(512)(128)(2,1)S(1)}, bf16[512]{0:T(512)(128)(2,1)}, u32[]{:S(2)}) copy-start(bf16[512]{0:T(512)(128)(2,1)} %param.19) | copy-start | bytes 3076
  6.5 8.3 %copy-start.24 = (bf16[512]{0:T(512)(128)(2,1)S(1)}, bf16[512]{0:T(512)(128)(2,1)}, u32[]{:S(2)}) copy-start(bf16[512]{0:T(512)(128)(2,1)} %param.20) | copy-start | bytes 3076
  6.6 71.8 %all-reduce.3.cloned.1.call-start = ((), (), s32[]{:S(2)}) async-start(), calls=%async_computation.5 | async-start | bytes 2621440 | tf_op jit(solution)/shard_map/psum | solution.py:99
  12.8 2.1 %copy-start.11 = (bf16[2,512,512]{2,1,0:T(8,128)(2,1)S(1)}, bf16[2,512,512]{2,1,0:T(8,128)(2,1)}, u32[]{:S(2)}) copy-start(bf16[2,512,512]{2,1,0:T(8,128)(2,1)} %param.22) | copy-start | bytes 3145732
  12.8 2.6 %copy-start.22 = (s32[8]{0:T(128)S(1)}, s32[8]{0:T(128)}, u32[]{:S(2)}) copy-start(s32[8]{0:T(128)} %param.26) | copy-start | bytes 100
  12.8 2.6 %copy-start.27 = (s32[8]{0:T(128)S(1)}, s32[8]{0:T(128)}, u32[]{:S(2)}) copy-start(s32[8]{0:T(128)} %param.27) | copy-start | bytes 100
  15.5 8.6 %copy-start.18 = (pred[64]{0:T(512)(128)(4,1)}, pred[64]{0:T(512)(128)(4,1)S(1)}, u32[]{:S(2)}) copy-start(pred[64]{0:T(512)(128)(4,1)S(1)} %get-tuple-element.32) | copy-start | bytes 196
  15.5 8.5 %copy-start.20 = (pred[64]{0:T(512)(128)(4,1)}, pred[64]{0:T(512)(128)(4,1)S(1)}, u32[]{:S(2)}) copy-start(pred[64]{0:T(512)(128)(4,1)S(1)} %get-tuple-element.33) | copy-start | bytes 196
  78.4 1.5 copy-start.14
  78.4 1.6 copy-start.15
  81.6 5.3 %copy-start.1 = (f32[4,64,8,512]{3,2,1,0:T(8,128)}, f32[4,64,8,512]{3,2,1,0:T(8,128)S(1)}, u32[]{:S(2)}) copy-start(f32[4,64,8,512]{3,2,1,0:T(8,128)S(1)} %get-tuple-element.37) | copy-start | bytes 12582916
  82.5 4.4 %copy-start.3 = (f32[4,64,8,512]{3,2,1,0:T(8,128)}, f32[4,64,8,512]{3,2,1,0:T(8,128)S(1)}, u32[]{:S(2)}) copy-start(f32[4,64,8,512]{3,2,1,0:T(8,128)S(1)} %get-tuple-element.35) | copy-start | bytes 12582916
  83.3 1.3 copy-start.6
  84.6 2.3 %copy-start.19 = (pred[64]{0:T(512)(128)(4,1)S(1)}, pred[64]{0:T(512)(128)(4,1)}, u32[]{:S(2)}) copy-start(pred[64]{0:T(512)(128)(4,1)} %copy-done.18) | copy-start | bytes 196
  84.6 2.4 %copy-start.21 = (pred[64]{0:T(512)(128)(4,1)S(1)}, pred[64]{0:T(512)(128)(4,1)}, u32[]{:S(2)}) copy-start(pred[64]{0:T(512)(128)(4,1)} %copy-done.20) | copy-start | bytes 196
  84.6 2.5 %copy-start.4 = (bf16[2,1024,4,128]{3,2,1,0:T(4,128)(2,1)S(1)}, bf16[2,1024,4,128]{3,2,1,0:T(4,128)(2,1)}, u32[]{:S(2)}) copy-start(bf16[2,1024,4,128]{3,2,1,0:T(4,128)(2,1)} %reshape.290) | copy-start | bytes 6291460
  86.9 1.7 copy-start.25
  86.9 1.7 copy-start.26
  88.7 1.5 copy-start.12
  91.8 15.7 %all-to-all-start.1 = ((f32[8,1,256]{2,1,0:T(1,128)}), f32[8,1,256]{2,1,0:T(1,128)S(1)}, u32[]{:S(2)}, u32[]{:S(2)}) async-start(f32[8,1,256]{2,1,0:T(1,128)} %reshape.303), calls=%async_computation.1 | async-start | bytes 16384 | tf_op jit(solution)/shard_map/all_to_all | solution.py:193
  95.3 3.6 %copy-start.2 = (f32[4,64,8,512]{3,2,1,0:T(8,128)S(1)}, f32[4,64,8,512]{3,2,1,0:T(8,128)}, u32[]{:S(2)}) copy-start(f32[4,64,8,512]{3,2,1,0:T(8,128)} %copy-done.1) | copy-start | bytes 12582916
  95.3 3.7 %copy-start.8 = (bf16[1,512,512]{1,2,0:T(8,128)(2,1)S(1)}, bf16[1,512,512]{1,2,0:T(8,128)(2,1)}, u32[]{:S(2)}) copy-start(bf16[1,512,512]{1,2,0:T(8,128)(2,1)} %copy.231) | copy-start | bytes 1572868
  100.6 1.0 copy-start.5
  101.6 4.8 %copy-start.7 = (f32[2,8,4,8,8]{3,4,1,2,0:T(8,128)S(1)}, f32[2,8,4,8,8]{3,4,1,2,0:T(8,128)}, u32[]{:S(2)}) copy-start(f32[2,8,4,8,8]{3,4,1,2,0:T(8,128)} %copy-done.6) | copy-start | bytes 49156
  103.0 3.4 %copy-start.16 = (f32[2,8,4,8]{3,1,2,0:T(8,128)S(1)}, f32[2,8,4,8]{3,1,2,0:T(8,128)}, u32[]{:S(2)}) copy-start(f32[2,8,4,8]{3,1,2,0:T(8,128)} %get-tuple-element.24) | copy-start | bytes 6148
  103.0 3.7 %copy-start.13 = (f32[1,64,4,8]{3,1,2,0:T(8,128)S(1)}, f32[1,64,4,8]{3,1,2,0:T(8,128)}, u32[]{:S(2)}) copy-start(f32[1,64,4,8]{3,1,2,0:T(8,128)} %copy-done.12) | copy-start | bytes 24580
  107.6 10.5 %all-to-all-start.2 = ((f32[8,1,256]{2,1,0:T(1,128)}), f32[8,1,256]{2,1,0:T(1,128)S(1)}, u32[]{:S(2)}, u32[]{:S(2)}) async-start(f32[8,1,256]{2,1,0:T(1,128)} %reshape.305), calls=%async_computation.2 | async-start | bytes 16384 | tf_op jit(solution)/shard_map/all_to_all | solution.py:194
  118.0 30.1 %all-to-all-start = ((f32[1,64,4,8,128]{4,3,2,0,1:T(8,128)}), f32[1,64,4,8,128]{4,3,2,0,1:T(8,128)S(1)}, u32[]{:S(2)}, u32[]{:S(2)}) async-start(f32[1,64,4,8,128]{4,3,2,0,1:T(8,128)} %copy.188), calls=%async_computation | async-start | bytes 2097152 | tf_op jit(solution)/shard_map/all_to_all | solution.py:195
  121.6 64.5 %reduce-scatter.2.cloned.1.call-start = ((), (), s32[]{:S(2)}) async-start(), calls=%async_computation.4 | async-start | bytes 393216 | tf_op jit(solution)/shard_map/reduce_scatter | solution.py:204
  148.6 1.3 collective-permute-start
  149.9 5.6 %collective-permute-start.1 = (bf16[16,4096]{1,0:T(8,128)(2,1)S(1)}, bf16[16,4096]{1,0:T(8,128)(2,1)S(1)}, u32[]{:S(2)}, u32[]{:S(2)}) collective-permute-start(bf16[16,4096]{1,0:T(8,128)(2,1)S(1)} %maximum_select_fusion.3), channel_id=1, source_target_pairs={{0,4},{1,5},{4,0},{5,1},{8,12},{9,13},{12,8},{13,9},{2,6},{3,7},{6... | collective-permute-start | bytes 393224 | tf_op jit(solution)/shard_map/ppermute | solution.py:17
  155.6 14.1 %collective-permute-start.2 = (bf16[32,4096]{1,0:T(8,128)(2,1)S(1)}, bf16[32,4096]{1,0:T(8,128)(2,1)S(1)}, u32[]{:S(2)}, u32[]{:S(2)}) collective-permute-start(bf16[32,4096]{1,0:T(8,128)(2,1)S(1)} %maximum_select_fusion.2), channel_id=1, source_target_pairs={{0,8},{1,9},{4,12},{5,13},{8,0},{9,1},{12,4},{13,5},{2,10},{3,11},... | collective-permute-start | bytes 786440 | tf_op jit(solution)/shard_map/ppermute | solution.py:17
Sparse Core Ops, SparseCore 0:
  14.9 63.4 all-reduce.2
  175.5 10.5 reduce-scatter.1
